TPU v7x, 512 devices: a whole 4x8x8 slice. The times are simulated.
512 devices in a mesh: rep: 16 (over y, core), tp: 32 (over z, x).
Axes of the slice: x: 4, y: 8, z: 8, core: 2. Of those that a mesh axis runs over, the one named last changes fastest.
Arguments:
- tokens: bfloat16 [8192, 8192], P('rep', 'tp'), may hold values from -6 to 6
- base_weight: bfloat16 [8192, 8192], P(None, 'tp'), may hold values from -0.0625 to 0.0625
- delta: bfloat16 [48, 64, 2, 128, 128], P('rep', 'tp'), may hold values from -0.375 to 0.375
- live_blocks: int32 [48, 64, 2], P(None, 'tp'), may hold values from 0 to 63, as said below
- row_variant: int32 [8192, 1], P('rep'), may hold values from 0 to 47; in each aligned block of 512 rows (0 to 511, 512 to 1023, ...) at most 21 rows name the same one
Outputs:
- projected: bfloat16 [8192, 8192], P('rep', 'tp')
Inputs may be any that keep to these rules, and one draw needn't show every extreme that they name: `live_blocks`: the 2 block rows listed for one variant and column block are distinct. `row_variant`: among the rows of one index of rep no variant appears more than 21 times, and some variant appears exactly 21 times.
All inputs are finite; a program needn't handle non-finite values.
Results may differ from a plain program's by a relative error of at most 0.0039.
Values may be sent and summed in bfloat16 or wider, within the bound.
A program may use at most 128 MiB of HBM per device.

v0:
```python
import jax
import jax.numpy as jnp
from jax import lax
from jax.sharding import PartitionSpec as P


def multiply(received, weight_tables):
    sources, local_variants, slot_count, feat_width = received.shape
    col_blocks = weight_tables.shape[1]
    block_size = weight_tables.shape[3]
    shaped = received.reshape(
        sources, local_variants, slot_count, col_blocks, feat_width // col_blocks
    )
    flat_weights = weight_tables.reshape(
        local_variants, col_blocks, feat_width // col_blocks, block_size
    )
    result = jnp.einsum(
        "auncf,ucfb->auncb", shaped, flat_weights, preferred_element_type=jnp.float32
    )
    return result.astype(jnp.bfloat16).reshape(
        sources, local_variants, slot_count, col_blocks * block_size
    )


def local(tokens, base_weight, delta, live_blocks, row_variant):
    rep_count = lax.axis_size("rep")
    local_variants = delta.shape[0]
    col_blocks = delta.shape[1]
    live_count = delta.shape[2]
    block_size = delta.shape[3]
    variants = local_variants * rep_count
    row_count = tokens.shape[0]
    capacity = max(2, 2 * row_count // variants)
    feat_width = col_blocks * live_count * block_size
    features_all = lax.all_gather(tokens, "tp", axis=1, tiled=True)
    base_part = jnp.dot(features_all, base_weight, preferred_element_type=jnp.float32)
    variant = row_variant[:, 0]
    onehot = (variant[:, None] == jnp.arange(variants, dtype=jnp.int32)[None, :]).astype(jnp.int32)
    row_rank = jnp.sum((jnp.cumsum(onehot, axis=0) - 1) * onehot, axis=1)
    slot_index = variant * capacity + row_rank
    tile_indices = jnp.take(live_blocks, variant, axis=0).reshape(
        row_count, col_blocks * live_count
    )
    blocks_view = features_all.reshape(row_count, features_all.shape[1] // block_size, block_size)
    picked = jnp.take_along_axis(blocks_view, tile_indices[:, :, None], axis=1).reshape(
        row_count, feat_width
    )
    outgoing = jnp.zeros((variants * capacity, feat_width), jnp.bfloat16).at[slot_index].set(picked)
    all_deltas = lax.all_gather(delta, "rep", axis=0, tiled=True)
    returned = multiply(outgoing.reshape(1, variants, capacity, feat_width), all_deltas)
    returned_flat = returned.reshape(variants * capacity, col_blocks * block_size)
    correction_summand = jnp.take(returned_flat, slot_index, axis=0)
    return (base_part + correction_summand.astype(jnp.float32)).astype(jnp.bfloat16)


def solution(mesh):
    placed = (
        P("rep", "tp"),
        P(None, "tp"),
        P("rep", "tp", None, None, None),
        P(None, "tp", None),
        P("rep", None),
    )
    return jax.shard_map(
        local, mesh=mesh, in_specs=placed, out_specs=P("rep", "tp"), check_vma=False
    )
```

profile of v0, /device:TPU:1, one launch (start us, length us, event | category | flops | bytes accessed | tf_op | source)
XLA Modules:
  0.0 194.5 jit_solution(5336732794186079991)
XLA Ops:
  6.5 0.0 all-gather.3.cloned.1.call-start
  6.5 0.7 all-gather.3.cloned.1.call-update
  7.3 0.0 all-gather.5.cloned.1.call-start
  7.3 0.7 all-gather.5.cloned.1.call-update
  8.0 0.7 fusion.9
  8.7 1.2 reduce-window.6
  9.9 0.2 slice_reduce_fusion
  10.2 0.8 copy.20
  11.0 0.8 fusion.8
  11.7 0.7 and_reduce_fusion
  12.5 2.1 %gather_fusion = s32[512,2,2]{2,1,0:T(2,128)S(1)} fusion(s32[48,2,2]{2,1,0:T(2,128)S(1)} %copy.20, s32[1024]{0:T(1024)S(1)} %pad_clamp_fusion.1), kind=kCustom, calls=%fused_computation | custom fusion | bytes 18432 | tf_op jit(solution)/shard_map/jit(_take)/gather | solution.py:41
  14.6 0.2 copy.21
  14.8 0.1 copy.24
  15.0 0.2 reshape.171
  15.2 0.2 copy.22
  15.4 105.8 %all-gather.3.cloned.1.call-done = bf16[512,8192]{1,0:T(8,128)(2,1)} async-done(((bf16[512,256]{1,0:T(8,128)(2,1)}), bf16[512,8192]{1,0:T(8,128)(2,1)}) %all-gather.3.cloned.1.call-update) | async-done | bytes 8388624 | tf_op jit(solution)/shard_map/all_gather | solution.py:35
  121.1 9.3 %copy.28 = bf16[64,8,64,128]{3,2,1,0:T(8,128)(2,1)} copy(bf16[64,8,64,128]{3,1,2,0:T(8,128)(2,1)} %bitcast.50) | data formatting | bytes 16777216
  130.4 24.5 %gather_fusion.2 = bf16[2048,128]{1,0:T(8,128)(2,1)S(1)} fusion(bf16[512,64,128]{2,1,0:T(8,128)(2,1)} %bitcast.48, s32[2048]{0:T(1024)S(1)} %reshape.171), kind=kCustom, calls=%fused_computation.2 | custom fusion | bytes 1064960 | tf_op jit(solution)/shard_map/jit(take_along_axis)/gather | solution.py:45
  155.0 1.6 broadcast_select_fusion
  156.6 2.7 %scatter_custom_fusion = bf16[1008,512]{1,0:T(8,128)(2,1)S(1)} fusion(s32[512]{0:T(512)S(1)} %bitcast.58, bf16[64,8,4,128]{3,2,1,0:T(4,128)(2,1)S(1)} %bitcast.52, bf16[]{:T(256)} %constant.50.clone.1), kind=kCustom, calls=%fused_computation.9 | custom fusion | bytes 1556482 | tf_op jit(solution)/shard_map/scatter | solution.py:48
  159.3 0.2 reshape.153
  159.6 14.2 %all-gather.5.cloned.1.call-done = bf16[48,2,2,128,128]{4,3,2,1,0:T(8,128)(2,1)} async-done(((bf16[3,2,2,128,128]{4,3,2,1,0:T(8,128)(2,1)}), bf16[48,2,2,128,128]{4,3,2,1,0:T(8,128)(2,1)}) %all-gather.5.cloned.1.call-update) | async-done | bytes 6291472 | tf_op jit(solution)/shard_map/all_gather | solution.py:49
  173.8 3.8 %fusion = bf16[1,48,21,2,128]{4,2,3,1,0:T(8,128)(2,1)S(1)} fusion(bf16[48,2,256,128]{3,2,1,0:T(8,128)(2,1)} %bitcast.51, bf16[48,21,2,256]{3,2,1,0:T(2,128)(2,1)S(1)} %reshape.153), kind=kOutput, calls=%fused_computation.5 | convolution fusion | flops 132378624 | bytes 7839744 | tf_op jit(solution)/shard_map/auncf,ucfb->auncb/dot_general | solution.py:17
  177.6 0.4 copy.26
  178.0 0.1 copy.39
  178.1 2.0 %gather_fusion.1 = bf16[512,256]{1,0:T(8,128)(2,1)S(1)} fusion(bf16[1008,256]{1,0:T(8,128)(2,1)S(1)} %bitcast.49, s32[1024]{0:T(1024)S(1)} %pad_clamp_fusion), kind=kCustom, calls=%fused_computation.1 | custom fusion | bytes 526336 | tf_op jit(solution)/shard_map/jit(_take)/gather | solution.py:52
  180.1 7.6 %fusion.1 = bf16[512,256]{1,0:T(8,128)(2,1)} fusion(bf16[512,8192]{1,0:T(8,128)(2,1)} %all-gather.3.cloned.1.call-done, bf16[8192,256]{1,0:T(8,128)(2,1)} %param.6, bf16[512,256]{1,0:T(8,128)(2,1)S(1)} %gather_fusion.1, pred[512]{0:T(512)(128)(4,1)S(1)} %get-tuple-element.9), kind=kOutput, calls=%fused_computation.7 | convolution fusion | flops 2148007936 | bytes 13107712 | tf_op jit(solution)/shard_map/dot_general | solution.py:36
  (8 shorter events, 0.1 us)
Async XLA Ops:
  6.5 114.6 %all-gather.3.cloned.1.call-start = ((), (), s32[]{:S(2)}) async-start(), calls=%async_computation | async-start | bytes 8650752 | tf_op jit(solution)/shard_map/all_gather | solution.py:35
  7.3 166.5 %all-gather.5.cloned.1.call-start = ((), (), s32[]{:S(2)}) async-start(), calls=%async_computation.1 | async-start | bytes 6684672 | tf_op jit(solution)/shard_map/all_gather | solution.py:49
Sparse Core Ops, SparseCore 0:
  10.4 110.7 all-gather.2
  123.3 50.4 all-gather.4
where the time goes:
time: 195 us
  waiting for transfers between devices  121 us (62%)
  local copies, waits for them, and re-layouts  43 us (22%)
  between operations  13.5 us (7%)
  matrix products  11.4 us (6%)
  other arithmetic  5.09 us (3%)
    all_gather x1, waiting for transfers between devices, local(): features_all = lax.all_gather(tokens, 'tp', axis=1, tiled=True)  106 us
    gather x3, local copies, waits for them, and re-layouts, local(): jnp.take_along_axis(blocks_view, tile_indices[:, :, None], axis=1)  24.8 us
    all_gather x1, waiting for transfers between devices, local(): all_deltas = lax.all_gather(delta, 'rep', axis=0, tiled=True)  14.2 us
    unnamed x3, local copies, waits for them, and re-layouts  10.2 us
    dot_general x1, matrix products, local(): jnp.dot(features_all, base_weight, preferred_element_type=jnp.float32)  7.61 us
  transfers between devices with their start and end apart: 2, of which 2 were waited for; matrix products, arithmetic and copies ran while one was open for 23% of the time, Pallas kernels for 0%

commit v1 on v0

v1 whole, which is shorter than its diff:
```python
import functools
import heapq

import jax
import jax.numpy as jnp
from jax import lax
from jax.experimental import pallas as pl
from jax.experimental.pallas import tpu as pltpu
from jax.sharding import PartitionSpec as P

NX, NZ, NY = 4, 8, 8
BLK = 128
SLOT = 24
HALVES = {"A": ((0, 96), (96, 208)), "B": ((208, 368), (368, 512))}
ROWS = {"A": (0, 208), "B": (208, 512)}
GROUP = 4
LANE_RATE, LATENCY = 46.5e3, 1.9


def token_forwards(part, dz, dx):
    full, (low, high) = ROWS[part], HALVES[part]

    def along_z():
        out = []
        if 0 <= dz < 3:
            out.append(("z+", full, dz + 1, dx))
        if -3 < dz <= 0:
            out.append(("z-", full, dz - 1, dx))
        if dz == 3:
            out.append(("z+", low, 4, dx))
        if dz == -3:
            out.append(("z-", high, 4, dx))
        return out

    def along_x():
        if dx == 0:
            return [("x+", full, dz, 1), ("x-", full, dz, -1)]
        if dx == 1:
            return [("x+", low, dz, 2)]
        if dx == -1:
            return [("x-", high, dz, 2)]
        return []

    if part == "A":
        return (along_x() if dz == 0 else []) + along_z()
    return (along_z() if dx == 0 else []) + along_x()


def delta_forwards(dy):
    full, low, high = (0, 12), (0, 6), (6, 12)
    out = []
    if 0 <= dy < 3:
        out.append(("y+", full, dy + 1))
    if -3 < dy <= 0:
        out.append(("y-", full, dy - 1))
    if dy == 3:
        out.append(("y+", low, 4))
    if dy == -3:
        out.append(("y-", high, 4))
    return out


def schedule():
    free, queue, order, numbers = {}, [], [], {}
    pending, count = {}, 0

    def send(now, kind, key, forward):
        nonlocal count
        link, rows, target = forward
        size = (rows[1] - rows[0]) * (512 if kind == "token" else 32768)
        end = max(now, free.get(link, 0.0)) + size / LANE_RATE
        free[link] = end
        number = numbers[kind] = numbers.get(kind, -1) + 1
        count += 1
        heapq.heappush(queue, (end + LATENCY, count, kind, target, rows, number))
        return (kind, link, rows, key, number)

    def release(now, kind, key):
        if kind == "token":
            forwards = [(f[0], f[1], (key[0], f[2], f[3])) for f in token_forwards(*key)]
        else:
            forwards = [(f[0], f[1], f[2]) for f in delta_forwards(key)]
        return [send(now, kind, key, f) for f in forwards]

    first = []
    for kind, key in (("token", ("B", 0, 0)), ("token", ("A", 0, 0)), ("delta", 0)):
        first += release(0.0, kind, key)
    while queue:
        now, _, kind, key, rows, number = heapq.heappop(queue)
        whole = ROWS[key[0]] if kind == "token" else (0, 12)
        have = pending.get((kind, key), 0) + rows[1] - rows[0]
        pending[(kind, key)] = have
        done = have == whole[1] - whole[0]
        order.append((now, kind, key, rows, number, done, release(now, kind, key) if done else []))
    return first, order, numbers["token"] + 1, numbers["delta"] + 1


def kernel(
    tokens, weight, delta, live, variant, out,
    feat, held, deltas, acc, picked, wanted, group_in, group_out, grouped,
    send_sem, recv_sem, dsend_sem, drecv_sem, psend_sem, precv_sem, local_sem,
):
    rep, tp = lax.axis_index("rep"), lax.axis_index("tp")
    z, x = tp // NX, tp % NX
    y, core = rep // 2, rep % 2
    neighbour = {
        "x+": (rep, z * NX + (x + 1) % NX),
        "x-": (rep, z * NX + (x + NX - 1) % NX),
        "z+": (rep, ((z + 1) % NZ) * NX + x),
        "z-": (rep, ((z + NZ - 1) % NZ) * NX + x),
        "y+": (((y + 1) % NY) * 2 + core, tp),
        "y-": (((y + NY - 1) % NY) * 2 + core, tp),
        "pair": (y * 2 + 1 - core, tp),
    }
    row_count, slots = acc.shape[0], grouped.shape[0]

    own = pltpu.make_async_copy(tokens, feat.at[tp], local_sem.at[0])
    own.start()
    load_weight = pltpu.make_async_copy(weight, held, local_sem.at[1])
    load_weight.start()
    own_delta = pltpu.make_async_copy(delta, deltas.at[pl.ds(rep * 12, 12)], local_sem.at[2])
    own_delta.start()

    barrier = pltpu.get_barrier_semaphore()
    for device in neighbour.values():
        pl.semaphore_signal(barrier, inc=1, device_id=device, device_id_type=pl.DeviceIdType.MESH)
    pl.semaphore_wait(barrier, len(neighbour))

    def shard_of(dz, dx):
        return ((z - dz + NZ) % NZ) * NX + (x - dx + NX) % NX

    def place(kind, key, rows):
        if kind == "token":
            return feat.at[shard_of(key[1], key[2]), pl.ds(rows[0], rows[1] - rows[0])]
        return deltas.at[pl.ds((((y - key + NY) % NY) * 2 + core) * 12 + rows[0], rows[1] - rows[0])]

    def remote(kind, source, target, number, device):
        sems = {
            "token": (send_sem, recv_sem),
            "delta": (dsend_sem, drecv_sem),
            "pair": (psend_sem, precv_sem),
        }[kind]
        return pltpu.make_async_remote_copy(
            src_ref=source,
            dst_ref=target,
            send_sem=sems[0].at[number],
            recv_sem=sems[1].at[number],
            device_id=device,
            device_id_type=pl.DeviceIdType.MESH,
        )

    started, pair_waits = [], []

    def send(step, from_input=False):
        kind, link, rows, key, number = step
        target = place(kind, key, rows)
        source = target
        if from_input:
            source = (tokens if kind == "token" else delta).at[pl.ds(rows[0], rows[1] - rows[0])]
        copy = remote(kind, source, target, number, neighbour[link])
        copy.start()
        started.append(copy)

    def to_pair(key, number, from_input=False):
        target = place("delta", key, (0, 12))
        copy = remote("pair", delta if from_input else target, target, number, neighbour["pair"])
        copy.start()
        started.append(copy)
        mirrored = deltas.at[pl.ds((((y - key + NY) % NY) * 2 + 1 - core) * 12, 12)]
        pair_waits.append(remote("pair", mirrored, mirrored, number, neighbour["pair"]))

    first, order, _, _ = schedule()
    for step in sorted(first, key=lambda s: (s[0] == "delta", (s[3][0] == "A") == (s[1][0] == "z")) if s[0] == "token" else (True, False)):
        send(step, True)
    to_pair(0, 0, True)

    names = variant[...].astype(jnp.float32)
    chunk = 128
    rank_row = jnp.zeros((1, row_count), jnp.float32)
    lane = lax.broadcasted_iota(jnp.int32, (chunk, row_count), 1)
    below = lax.broadcasted_iota(jnp.int32, (chunk, row_count), 0)
    for start in range(0, row_count, chunk):
        here = below + start
        column = jnp.sum(jnp.where(lane == here, names, 0.0), axis=1, keepdims=True)
        same = jnp.where(column == names, 1.0, 0.0)
        rank = jnp.sum(jnp.where(lane < here, same, 0.0), axis=1, keepdims=True)
        rank_row += jnp.sum(jnp.where(here < lane, same, 0.0), axis=0, keepdims=True)
        slot = column * SLOT + rank
        places = lax.broadcasted_iota(jnp.int32, (chunk, slots), 1).astype(jnp.float32)
        group_out[pl.ds(start, chunk)] = jnp.where(places == slot, 1.0, 0.0).astype(jnp.bfloat16)
        held_names = lax.broadcasted_iota(jnp.int32, (chunk, live.shape[2]), 1).astype(jnp.float32)
        for c in range(2):
            for k in range(2):
                listed = live[c, pl.ds(k, 1)].astype(jnp.float32)
                want = jnp.sum(jnp.where(held_names == column, listed, 0.0), axis=1, keepdims=True)
                lanes = pl.ds((c * 2 + k) * BLK, BLK)
                wanted[pl.ds(start, chunk), lanes] = jnp.broadcast_to(want, (chunk, BLK)).astype(jnp.bfloat16)
    slot_row = names * SLOT + rank_row
    acc[...] = jnp.zeros_like(acc)
    picked[...] = jnp.zeros_like(picked)

    @pl.loop(0, slots // 128)
    def _(i):
        places = (lax.broadcasted_iota(jnp.int32, (128, row_count), 0) + i * 128).astype(jnp.float32)
        group_in[pl.ds(i * 128, 128)] = jnp.where(places == slot_row, 1.0, 0.0).astype(jnp.bfloat16)

    def multiply(part, keys):
        low, high = ROWS[part]
        rows = pl.ds(low, high - low)
        packed = 0
        for key in reversed(keys):
            packed = packed * 32 + (key[1] % NZ) * NX + key[2] % NX

        def body(_, code):
            shard = shard_of(code % 32 // NX, code % NX)
            block = feat[shard, rows]
            table = held[pl.ds(pl.multiple_of(shard * 256, 256), 256)]
            acc[rows] += jnp.dot(block, table, preferred_element_type=jnp.float32)
            for j in range(4):
                lanes = pl.ds(j * BLK, BLK)
                want, value = wanted[rows, lanes], picked[rows, lanes]
                for h in range(2):
                    name = (shard * 2 + h).astype(jnp.float32)
                    name = jnp.full((high - low, BLK), name, jnp.float32).astype(jnp.bfloat16)
                    value = jnp.where(want == name, block[:, h * BLK:(h + 1) * BLK], value)
                picked[rows, lanes] = value
            return code // 32

        lax.fori_loop(0, len(keys), body, jnp.int32(packed))

    own.wait()
    own_delta.wait()
    load_weight.wait()
    waiting = {"A": [("A", 0, 0)], "B": [("B", 0, 0)]}
    pairs = 1
    for _, kind, key, rows, number, done, sends in order:
        slot = place(kind, key, rows)
        remote(kind, slot, slot, number, neighbour["pair"]).wait_recv()
        for step in sends:
            send(step)
        if kind == "delta" and done:
            to_pair(key, pairs)
            pairs += 1
        if kind == "token" and done:
            waiting[key[0]].append(key)
            if len(waiting[key[0]]) == GROUP:
                multiply(key[0], waiting[key[0]])
                waiting[key[0]] = []
    for part in ("A", "B"):
        if waiting[part]:
            multiply(part, waiting[part])
    for copy in pair_waits:
        copy.wait_recv()

    step_rows, step_variants = SLOT * 6, 6

    @pl.loop(0, slots // step_rows)
    def _(i):
        at = pl.ds(pl.multiple_of(i * step_rows, 16), step_rows)
        chosen = jnp.dot(group_in[at], picked[...], preferred_element_type=jnp.float32)
        for u in range(step_variants):
            for c in range(2):
                mine = chosen[u * SLOT:(u + 1) * SLOT, c * 256:(c + 1) * 256].astype(jnp.bfloat16)
                table = deltas[pl.ds((i * step_variants + u) * 4 + c * 2, 2)].reshape(256, BLK)
                grouped[pl.ds(pl.multiple_of(i * step_rows, 8) + u * SLOT, SLOT), pl.ds(c * BLK, BLK)] = jnp.dot(
                    mine, table, preferred_element_type=jnp.float32
                )

    change = jnp.dot(
        group_out[...], grouped[...].astype(jnp.bfloat16), preferred_element_type=jnp.float32
    )
    out[...] = (acc[...] + change).astype(jnp.bfloat16)
    for copy in started:
        copy.wait_send()


def local(tokens, base_weight, delta, live_blocks, row_variant):
    rows, width = tokens.shape
    variants = live_blocks.shape[0]
    blocks = delta.shape[0] * 4
    _, _, token_sends, delta_sends = schedule()
    anywhere, vmem = pl.BlockSpec(memory_space=pl.ANY), pl.BlockSpec(memory_space=pltpu.VMEM)
    dma = pltpu.SemaphoreType.DMA
    return pl.pallas_call(
        kernel,
        out_shape=jax.ShapeDtypeStruct((rows, width), jnp.bfloat16),
        in_specs=[anywhere, anywhere, anywhere, vmem, vmem],
        out_specs=vmem,
        scratch_shapes=[
            pltpu.VMEM((NX * NZ, rows, width), jnp.bfloat16),
            pltpu.VMEM(base_weight.shape, jnp.bfloat16),
            pltpu.VMEM((blocks * NY * 2, BLK, BLK), jnp.bfloat16),
            pltpu.VMEM((rows, width), jnp.float32),
            pltpu.VMEM((rows, 4 * BLK), jnp.bfloat16),
            pltpu.VMEM((rows, 4 * BLK), jnp.bfloat16),
            pltpu.VMEM((variants * SLOT, rows), jnp.bfloat16),
            pltpu.VMEM((rows, variants * SLOT), jnp.bfloat16),
            pltpu.VMEM((variants * SLOT, width), jnp.float32),
            dma((token_sends,)),
            dma((token_sends,)),
            dma((delta_sends,)),
            dma((delta_sends,)),
            dma((NY,)),
            dma((NY,)),
            dma((3,)),
        ],
        compiler_params=pltpu.CompilerParams(
            collective_id=0, has_side_effects=True, vmem_limit_bytes=60 * 1024 * 1024
        ),
    )(
        tokens,
        base_weight,
        delta.reshape(blocks, BLK, BLK),
        jnp.transpose(live_blocks, (1, 2, 0)),
        row_variant.reshape(1, rows),
    )


def solution(mesh):
    placed = (
        P("rep", "tp"),
        P(None, "tp"),
        P("rep", "tp", None, None, None),
        P(None, "tp", None),
        P("rep", None),
    )
    return jax.shard_map(
        local, mesh=mesh, in_specs=placed, out_specs=P("rep", "tp"), check_vma=False
    )
```

time: 195 us -> 71 us (0.36)
  the two profiles are of different devices: /device:TPU:1 before, /device:TPU:24 now
where the time goes in v1:
time: 71 us; the launch traced here: 70.9 us
  Pallas kernels  69.2 us (97%)
  local copies, waits for them, and re-layouts  1.67 us (2%)
    pallas_call x1, Pallas kernels, local(): pl.pallas_call(kernel, out_shape=jax.ShapeDtypeStruct((rows, width), jnp....  69.2 us
    unnamed x1, local copies, waits for them, and re-layouts  1.67 us

profile of v1, /device:TPU:24, one launch (start us, length us, event | category | flops | bytes accessed | tf_op | source)
XLA Modules:
  0.0 70.9 jit_solution(2324982863183424848)
XLA Ops:
  0.0 69.2 %shard_map.55 = bf16[512,256]{1,0:T(8,128)(2,1)} custom-call(bf16[512,256]{1,0:T(8,128)(2,1)} %tokens.1, bf16[8192,256]{1,0:T(8,128)(2,1)} %weight.1, bf16[12,128,128]{2,1,0:T(8,128)(2,1)} %bitcast.3, s32[2,2,48]{2,1,0:T(2,128)} %bitcast.4, s32[1,512]{1,0:T(1,128)} %bitcast.5), custom_call_target="tpu_custom_call" | custom-call | tf_op jit(solution)/shard_map/pallas_call | solution.py:284
  69.2 1.7 %copy.7 = bf16[512,256]{1,0:T(8,128)(2,1)} copy(bf16[512,256]{1,0:T(8,128)(2,1)} %shard_map.55) | data formatting | bytes 524288

commit v2 on v1

--- a/solution.py
+++ b/solution.py
@@ -1,5 +1,5 @@
-import functools
 import heapq
+import itertools
 
 import jax
 import jax.numpy as jnp
@@ -11,14 +11,15 @@
 NX, NZ, NY = 4, 8, 8
 BLK = 128
 SLOT = 24
-HALVES = {"A": ((0, 96), (96, 208)), "B": ((208, 368), (368, 512))}
 ROWS = {"A": (0, 208), "B": (208, 512)}
 GROUP = 4
 LANE_RATE, LATENCY = 46.5e3, 1.9
 
 
 def token_forwards(part, dz, dx):
-    full, (low, high) = ROWS[part], HALVES[part]
+    full = ROWS[part]
+    middle = 96 if part == "A" else 352 if dx and dz % 2 else 368
+    low, high = (full[0], middle), (middle, full[1])
 
     def along_z():
         out = []
@@ -61,43 +62,49 @@
 
 
 def schedule():
-    free, queue, order, numbers = {}, [], [], {}
-    pending, count = {}, 0
-
-    def send(now, kind, key, forward):
-        nonlocal count
-        link, rows, target = forward
-        size = (rows[1] - rows[0]) * (512 if kind == "token" else 32768)
-        end = max(now, free.get(link, 0.0)) + size / LANE_RATE
-        free[link] = end
-        number = numbers[kind] = numbers.get(kind, -1) + 1
-        count += 1
-        heapq.heappush(queue, (end + LATENCY, count, kind, target, rows, number))
-        return (kind, link, rows, key, number)
+    sent, waiting, free, events, arrivals, have, numbers = {}, {}, {}, [], [], {}, {}
+    count = itertools.count()
 
     def release(now, kind, key):
         if kind == "token":
             forwards = [(f[0], f[1], (key[0], f[2], f[3])) for f in token_forwards(*key)]
         else:
-            forwards = [(f[0], f[1], f[2]) for f in delta_forwards(key)]
-        return [send(now, kind, key, f) for f in forwards]
-
-    first = []
-    for kind, key in (("token", ("B", 0, 0)), ("token", ("A", 0, 0)), ("delta", 0)):
-        first += release(0.0, kind, key)
-    while queue:
-        now, _, kind, key, rows, number = heapq.heappop(queue)
-        whole = ROWS[key[0]] if kind == "token" else (0, 12)
-        have = pending.get((kind, key), 0) + rows[1] - rows[0]
-        pending[(kind, key)] = have
-        done = have == whole[1] - whole[0]
-        order.append((now, kind, key, rows, number, done, release(now, kind, key) if done else []))
-    return first, order, numbers["token"] + 1, numbers["delta"] + 1
+            forwards = delta_forwards(key)
+        for link, rows, target in forwards:
+            later = kind == "token" and (key[0] == "A") != (link[0] == "x")
+            number = numbers[kind] = numbers.get(kind, -1) + 1
+            heapq.heappush(waiting.setdefault(link, []), (later, now, next(count), (kind, rows, key, number), target))
+            heapq.heappush(events, (max(now, free.get(link, 0.0)), next(count), link, None))
+
+    release(0.0, "token", ("A", 0, 0))
+    release(0.0, "token", ("B", 0, 0))
+    release(0.0, "delta", 0)
+    while events:
+        now, _, link, arrival = heapq.heappop(events)
+        if arrival is None:
+            if free.get(link, 0.0) > now or not waiting[link]:
+                continue
+            _, _, _, step, target = heapq.heappop(waiting[link])
+            kind, rows, _, number = step
+            end = now + (rows[1] - rows[0]) * (512 if kind == "token" else 32768) / LANE_RATE
+            free[link] = end
+            sent.setdefault(link, []).append(step)
+            heapq.heappush(events, (end, next(count), link, None))
+            heapq.heappush(events, (end + LATENCY, next(count), link, (kind, target, rows, number)))
+        else:
+            kind, key, rows, number = arrival
+            whole = ROWS[key[0]] if kind == "token" else (0, 12)
+            have[kind, key] = have.get((kind, key), 0) + rows[1] - rows[0]
+            done = have[kind, key] == whole[1] - whole[0]
+            arrivals.append((kind, key, rows, number, done))
+            if done:
+                release(now, kind, key)
+    return sent, arrivals, numbers["token"] + 1, numbers["delta"] + 1
 
 
 def kernel(
     tokens, weight, delta, live, variant, out,
-    feat, held, deltas, acc, picked, wanted, group_in, group_out, grouped,
+    feat, held, deltas, acc, picked, wanted, group_in, group_out, chosen, grouped,
     send_sem, recv_sem, dsend_sem, drecv_sem, psend_sem, precv_sem, local_sem,
 ):
     rep, tp = lax.axis_index("rep"), lax.axis_index("tp")
@@ -151,15 +158,21 @@
 
     started, pair_waits = [], []
 
-    def send(step, from_input=False):
-        kind, link, rows, key, number = step
-        target = place(kind, key, rows)
-        source = target
-        if from_input:
-            source = (tokens if kind == "token" else delta).at[pl.ds(rows[0], rows[1] - rows[0])]
-        copy = remote(kind, source, target, number, neighbour[link])
-        copy.start()
-        started.append(copy)
+    sent, arrivals, _, _ = schedule()
+    ready = {("token", ("A", 0, 0)), ("token", ("B", 0, 0)), ("delta", 0)}
+    own_keys = set(ready)
+
+    def send_ready():
+        for link, steps in sent.items():
+            while steps and (steps[0][0], steps[0][2]) in ready:
+                kind, rows, key, number = steps.pop(0)
+                target = place(kind, key, rows)
+                source = target
+                if (kind, key) in own_keys:
+                    source = (tokens if kind == "token" else delta).at[pl.ds(rows[0], rows[1] - rows[0])]
+                copy = remote(kind, source, target, number, neighbour[link])
+                copy.start()
+                started.append(copy)
 
     def to_pair(key, number, from_input=False):
         target = place("delta", key, (0, 12))
@@ -169,9 +182,7 @@
         mirrored = deltas.at[pl.ds((((y - key + NY) % NY) * 2 + 1 - core) * 12, 12)]
         pair_waits.append(remote("pair", mirrored, mirrored, number, neighbour["pair"]))
 
-    first, order, _, _ = schedule()
-    for step in sorted(first, key=lambda s: (s[0] == "delta", (s[3][0] == "A") == (s[1][0] == "z")) if s[0] == "token" else (True, False)):
-        send(step, True)
+    send_ready()
     to_pair(0, 0, True)
 
     names = variant[...].astype(jnp.float32)
@@ -232,44 +243,45 @@
     own_delta.wait()
     load_weight.wait()
     waiting = {"A": [("A", 0, 0)], "B": [("B", 0, 0)]}
+    left = {"A": NX * NZ, "B": NX * NZ}
     pairs = 1
-    for _, kind, key, rows, number, done, sends in order:
+    for kind, key, rows, number, done in arrivals:
         slot = place(kind, key, rows)
         remote(kind, slot, slot, number, neighbour["pair"]).wait_recv()
-        for step in sends:
-            send(step)
-        if kind == "delta" and done:
+        if not done:
+            continue
+        ready.add((kind, key))
+        send_ready()
+        if kind == "delta":
             to_pair(key, pairs)
             pairs += 1
-        if kind == "token" and done:
-            waiting[key[0]].append(key)
-            if len(waiting[key[0]]) == GROUP:
-                multiply(key[0], waiting[key[0]])
-                waiting[key[0]] = []
-    for part in ("A", "B"):
-        if waiting[part]:
-            multiply(part, waiting[part])
+            continue
+        waiting[key[0]].append(key)
+        size = len(waiting[key[0]])
+        if size == min(GROUP, max(1, left[key[0]] // 2)):
+            multiply(key[0], waiting[key[0]])
+            left[key[0]] -= size
+            waiting[key[0]] = []
     for copy in pair_waits:
         copy.wait_recv()
 
-    step_rows, step_variants = SLOT * 6, 6
-
-    @pl.loop(0, slots // step_rows)
+    chosen[...] = jnp.dot(group_in[...], picked[...], preferred_element_type=jnp.float32)
+    step = 12
+
+    @pl.loop(0, slots // (SLOT * step))
     def _(i):
-        at = pl.ds(pl.multiple_of(i * step_rows, 16), step_rows)
-        chosen = jnp.dot(group_in[at], picked[...], preferred_element_type=jnp.float32)
-        for u in range(step_variants):
+        for u in range(step):
+            at = pl.ds(pl.multiple_of(i * (SLOT * step), 8) + u * SLOT, SLOT)
             for c in range(2):
-                mine = chosen[u * SLOT:(u + 1) * SLOT, c * 256:(c + 1) * 256].astype(jnp.bfloat16)
-                table = deltas[pl.ds((i * step_variants + u) * 4 + c * 2, 2)].reshape(256, BLK)
-                grouped[pl.ds(pl.multiple_of(i * step_rows, 8) + u * SLOT, SLOT), pl.ds(c * BLK, BLK)] = jnp.dot(
-                    mine, table, preferred_element_type=jnp.float32
-                )
-
-    change = jnp.dot(
-        group_out[...], grouped[...].astype(jnp.bfloat16), preferred_element_type=jnp.float32
-    )
-    out[...] = (acc[...] + change).astype(jnp.bfloat16)
+                mine = chosen[at, pl.ds(c * 256, 256)].astype(jnp.bfloat16)
+                table = deltas[pl.ds((i * step + u) * 4 + c * 2, 2)].reshape(256, BLK)
+                grouped[at, pl.ds(c * BLK, BLK)] = jnp.dot(mine, table, preferred_element_type=jnp.float32)
+
+    changes = grouped[...].astype(jnp.bfloat16)
+    for start in range(0, row_count, 256):
+        rows = pl.ds(start, 256)
+        change = jnp.dot(group_out[rows], changes, preferred_element_type=jnp.float32)
+        out[rows] = (acc[rows] + change).astype(jnp.bfloat16)
     for copy in started:
         copy.wait_send()
 
@@ -279,7 +291,7 @@
     variants = live_blocks.shape[0]
     blocks = delta.shape[0] * 4
     _, _, token_sends, delta_sends = schedule()
-    anywhere, vmem = pl.BlockSpec(memory_space=pl.ANY), pl.BlockSpec(memory_space=pltpu.VMEM)
+    anywhere, vmem = pl.BlockSpec(memory_space=pltpu.HBM), pl.BlockSpec(memory_space=pltpu.VMEM)
     dma = pltpu.SemaphoreType.DMA
     return pl.pallas_call(
         kernel,
@@ -295,6 +307,7 @@
             pltpu.VMEM((rows, 4 * BLK), jnp.bfloat16),
             pltpu.VMEM((variants * SLOT, rows), jnp.bfloat16),
             pltpu.VMEM((rows, variants * SLOT), jnp.bfloat16),
+            pltpu.VMEM((variants * SLOT, 4 * BLK), jnp.float32),
             pltpu.VMEM((variants * SLOT, width), jnp.float32),
             dma((token_sends,)),
             dma((token_sends,)),
@@ -305,7 +318,7 @@
             dma((3,)),
         ],
         compiler_params=pltpu.CompilerParams(
-            collective_id=0, has_side_effects=True, vmem_limit_bytes=60 * 1024 * 1024
+            collective_id=0, has_side_effects=True, vmem_limit_bytes=62 * 1024 * 1024
         ),
     )(
         tokens,

time: 71 us -> 68.9 us (0.970)
  the two profiles are of different devices: /device:TPU:24 before, /device:TPU:2 now
where the time goes in v2:
time: 68.9 us; the launch traced here: 68.7 us
  Pallas kernels  67 us (97%)
  local copies, waits for them, and re-layouts  1.67 us (2%)
    pallas_call x1, Pallas kernels, local(): pl.pallas_call(kernel, out_shape=jax.ShapeDtypeStruct((rows, width), jnp....  67 us
    unnamed x1, local copies, waits for them, and re-layouts  1.67 us

profile of v2, /device:TPU:2, one launch (start us, length us, event | category | flops | bytes accessed | tf_op | source)
XLA Modules:
  0.0 68.7 jit_solution(18369903913339465148)
XLA Ops:
  0.0 67.0 %shard_map.55 = bf16[512,256]{1,0:T(8,128)(2,1)} custom-call(bf16[512,256]{1,0:T(8,128)(2,1)} %tokens.1, bf16[8192,256]{1,0:T(8,128)(2,1)} %weight.1, bf16[12,128,128]{2,1,0:T(8,128)(2,1)} %bitcast.3, s32[2,2,48]{2,1,0:T(2,128)} %bitcast.4, s32[1,512]{1,0:T(1,128)} %bitcast.5), custom_call_target="tpu_custom_call" | custom-call | tf_op jit(solution)/shard_map/pallas_call | solution.py:296
  67.0 1.7 %copy.7 = bf16[512,256]{1,0:T(8,128)(2,1)} copy(bf16[512,256]{1,0:T(8,128)(2,1)} %shard_map.55) | data formatting | bytes 524288

commit v3 on v2

--- a/solution.py
+++ b/solution.py
@@ -12,8 +12,8 @@
 BLK = 128
 SLOT = 24
 ROWS = {"A": (0, 208), "B": (208, 512)}
-GROUP = 4
-LANE_RATE, LATENCY = 46.5e3, 1.9
+GROUP = 2
+LANE_RATE, LATENCY = 44.0e3, 3.0
 
 
 def token_forwards(part, dz, dx):
@@ -71,20 +71,19 @@
         else:
             forwards = delta_forwards(key)
         for link, rows, target in forwards:
-            later = kind == "token" and (key[0] == "A") != (link[0] == "x")
             number = numbers[kind] = numbers.get(kind, -1) + 1
-            heapq.heappush(waiting.setdefault(link, []), (later, now, next(count), (kind, rows, key, number), target))
+            heapq.heappush(waiting.setdefault(link, []), (now, next(count), (kind, rows, key, number), target))
             heapq.heappush(events, (max(now, free.get(link, 0.0)), next(count), link, None))
 
+    release(0.0, "token", ("B", 0, 0))
     release(0.0, "token", ("A", 0, 0))
-    release(0.0, "token", ("B", 0, 0))
     release(0.0, "delta", 0)
     while events:
         now, _, link, arrival = heapq.heappop(events)
         if arrival is None:
             if free.get(link, 0.0) > now or not waiting[link]:
                 continue
-            _, _, _, step, target = heapq.heappop(waiting[link])
+            _, _, step, target = heapq.heappop(waiting[link])
             kind, rows, _, number = step
             end = now + (rows[1] - rows[0]) * (512 if kind == "token" else 32768) / LANE_RATE
             free[link] = end
@@ -295,7 +294,7 @@
     dma = pltpu.SemaphoreType.DMA
     return pl.pallas_call(
         kernel,
-        out_shape=jax.ShapeDtypeStruct((rows, width), jnp.bfloat16),
+        out_shape=pltpu.VMEM((rows, width), jnp.bfloat16),
         in_specs=[anywhere, anywhere, anywhere, vmem, vmem],
         out_specs=vmem,
         scratch_shapes=[

time: 68.9 us -> 66.1 us (0.959)
  Pallas kernels: 67 us -> 65.2 us
  local copies, waits for them, and re-layouts: 1.67 us -> 0.71 us
    pallas_call x1, Pallas kernels: 67 us -> 65.2 us  [local(): pl.pallas_call(kernel, out_shape=pltpu.VMEM((rows, width), jnp.bfloat16),...]
    unnamed x1, local copies, waits for them, and re-layouts: 1.67 us -> 0.71 us
where the time goes in v3:
time: 66.1 us; the launch traced here: 66 us
  Pallas kernels  65.2 us (99%)
  local copies, waits for them, and re-layouts  0.71 us (1%)
    pallas_call x1, Pallas kernels, local(): pl.pallas_call(kernel, out_shape=pltpu.VMEM((rows, width), jnp.bfloat16),...  65.2 us

profile of v3, /device:TPU:2, one launch (start us, length us, event | category | flops | bytes accessed | tf_op | source)
XLA Modules:
  0.0 66.0 jit_solution(3616417221683424408)
XLA Ops:
  0.0 65.2 %shard_map.55 = bf16[512,256]{1,0:T(8,128)(2,1)S(1)} custom-call(bf16[512,256]{1,0:T(8,128)(2,1)} %tokens.1, bf16[8192,256]{1,0:T(8,128)(2,1)} %weight.1, bf16[12,128,128]{2,1,0:T(8,128)(2,1)} %bitcast.3, s32[2,2,48]{2,1,0:T(2,128)} %bitcast.4, s32[1,512]{1,0:T(1,128)} %bitcast.5), custom_call_target="tpu_custom_call" | custom-call | tf_op jit(solution)/shard_map/pallas_call | solution.py:295
  65.3 0.7 %copy.7 = bf16[512,256]{1,0:T(8,128)(2,1)} copy(bf16[512,256]{1,0:T(8,128)(2,1)S(1)} %shard_map.55) | data formatting | bytes 524288
